TPU v7x, 32 devices: a whole 2x2x4 slice. The times are simulated.
32 devices in a mesh: gx: 8 (over z, y), gz: 4 (over x, core).
Axes of the slice: x: 2, y: 2, z: 4, core: 2. Of those that a mesh axis runs over, the one named last changes fastest.
Arguments:
- volume: float32 [256, 64, 1024], P('gz', None, 'gx'), may hold values from -96 to 96
- centers: float32 [8], replicated, may hold values from -1.5 to 1.5
- sharpness: float32 [8], replicated, may hold values from 0.5 to 4
- extinction: float32 [8], replicated, may hold values from 0.2 to 3
- colors: float32 [3, 8], replicated, may hold values from 0 to 1
Outputs:
- image_tiles: float32 [4, 64, 1024], P(None, 'gz', 'gx')
All inputs are finite; a program needn't handle non-finite values.
Results may differ from a plain program's by a relative error of at most 0.00002.
Values sent between devices are 32-bit elements; how exact they have to be, the bound alone decides.
A program may use at most 64 MiB of HBM per device.

v0:
```python
import math

import jax
import jax.numpy as jnp
from jax import lax
from jax.sharding import PartitionSpec as P


def padded_2(cells, sides, width):
    for axis, dim in sides:
        count = lax.axis_size(axis)
        ends = count - 1
        head = lax.slice_in_dim(cells, 0, width, axis=dim)
        tail = lax.slice_in_dim(cells, cells.shape[dim] - width, cells.shape[dim], axis=dim)
        cells = jnp.concatenate(
            [
                lax.ppermute(tail, axis, [(i, (i + 1) % count) for i in range(ends)]),
                cells,
                lax.ppermute(head, axis, [((i + 1) % count, i) for i in range(ends)]),
            ],
            axis=dim,
        )
    return cells


def tap_weights():
    raw = [math.exp(-(j * j) / 8.0) for j in range(-4, 5)]
    whole = sum(raw)
    return [value / whole for value in raw]


def valid_pass(field, axis, count):
    weights = tap_weights()
    total = weights[0] * lax.slice_in_dim(field, 0, count, axis=axis)
    for offset in range(1, 9):
        total = total + weights[offset] * lax.slice_in_dim(field, offset, offset + count, axis=axis)
    return total


def padded_pass(field, axis):
    widths = [(0, 0), (0, 0), (0, 0)]
    widths[axis] = (4, 4)
    return valid_pass(jnp.pad(field, widths), axis, field.shape[axis])


def transfer(density, centers, sharpness, extinction, colors):
    sigma = jnp.zeros_like(density)
    emits = [jnp.zeros_like(density), jnp.zeros_like(density), jnp.zeros_like(density)]
    for comp in range(centers.shape[0]):
        offset = density - centers[comp]
        bump = jnp.exp(-sharpness[comp] * offset * offset)
        sigma = sigma + extinction[comp] * bump
        for chan in range(3):
            emits[chan] = emits[chan] + colors[chan, comp] * bump
    return (sigma, emits)


def over_blend(front, back):
    color = front[:3] + front[3:4] * back[:3]
    return jnp.concatenate([color, front[3:4] * back[3:4]], axis=0)


def on_device(volume, centers, sharpness, extinction, colors):
    depth_cells = volume.shape[0]
    columns = volume.shape[2]
    rows = volume.shape[1]
    padded = padded_2(volume, (("gx", 2), ("gz", 0)), 4)
    smoothed = valid_pass(padded, 0, depth_cells)
    smoothed = valid_pass(smoothed, 2, columns)
    density = padded_pass(smoothed, 1)
    sigma, emits = transfer(density, centers, sharpness, extinction, colors)
    tau = sigma / jnp.float32(depth_cells * lax.axis_size("gz"))
    cumul = jnp.cumsum(tau, axis=0)
    before = cumul - tau
    weight = jnp.exp(-before) * -jnp.expm1(-tau)
    planes = [jnp.sum(weight * emits[chan], axis=0) for chan in range(3)]
    planes.append(jnp.exp(-cumul[-1]))
    partial_image = jnp.stack(planes, axis=0)
    depth_count = lax.axis_size("gz")
    row_block = rows // depth_count
    blocks = partial_image.reshape(4, depth_count, row_block, columns)
    moved = lax.all_to_all(blocks, "gz", split_axis=1, concat_axis=0, tiled=True)
    pieces = moved.reshape(depth_count, 4, row_block, columns)
    start = jnp.concatenate(
        [
            jnp.zeros((3, row_block, columns), jnp.float32),
            jnp.ones((1, row_block, columns), jnp.float32),
        ],
        axis=0,
    )

    def front_to_back(carry, piece):
        return (over_blend(carry, piece), None)

    result, unused = lax.scan(front_to_back, start, pieces)
    return result


def solution(mesh):
    return jax.shard_map(
        on_device,
        mesh=mesh,
        in_specs=(P("gz", None, "gx"), P(), P(), P(), P()),
        out_specs=P(None, "gz", "gx"),
        check_vma=False,
    )
```

profile of v0, /device:TPU:1, one launch (start us, length us, event | category | flops | bytes accessed | tf_op | source)
XLA Modules:
  0.0 140.6 jit_solution(5850149380388390663)
XLA Ops:
  0.0 4.4 %fusion.46 = (f32[64,64,4]{2,1,0:T(8,128)S(1)}, f32[64,64,4]{2,1,0:T(8,128)}) fusion(f32[64,64,128]{2,1,0:T(8,128)} %param.7), kind=kLoop, calls=%fused_computation.92 | loop fusion | bytes 262144 | tf_op jit(solution)/shard_map/slice | solution.py:14
  4.4 2.3 %copy.13 = f32[64,64,4]{1,0,2:T(8,128)S(1)} copy(f32[64,64,4]{2,1,0:T(8,128)} %get-tuple-element.38) | data formatting | bytes 131072
  6.7 1.3 collective-permute-start.1
  8.1 0.7 copy.12
  8.8 4.6 %collective-permute-start = (f32[64,64,4]{1,0,2:T(8,128)S(1)}, f32[64,64,4]{1,0,2:T(8,128)S(1)}, u32[]{:S(2)}, u32[]{:S(2)}) collective-permute-start(f32[64,64,4]{1,0,2:T(8,128)S(1)} %copy.12), channel_id=1, source_target_pairs={{0,4},{4,8},{8,12},{12,16},{16,20},{20,24},{24,28},{1,5},{5,9},{9,... | collective-permute-start | bytes 196616 | tf_op jit(solution)/shard_map/ppermute | solution.py:17
  13.4 0.7 fusion.49
  14.1 0.7 fusion.50
  14.7 0.7 fusion.51
  15.4 0.0 collective-permute-done.1
  15.4 2.1 %copy.10 = f32[64,64,4]{2,1,0:T(8,128)} copy(f32[64,64,4]{1,0,2:T(8,128)S(1)} %collective-permute-done.1) | data formatting | bytes 131072 | tf_op jit(solution)/shard_map/ppermute | solution.py:19
  17.5 0.2 collective-permute-done
  17.6 2.1 %copy.9 = f32[64,64,4]{2,1,0:T(8,128)} copy(f32[64,64,4]{1,0,2:T(8,128)S(1)} %collective-permute-done) | data formatting | bytes 131072 | tf_op jit(solution)/shard_map/ppermute | solution.py:17
  19.8 4.1 %pad_maximum_fusion.2 = f32[64,64,136]{2,1,0:T(8,128)S(1)} fusion(f32[64,64,4]{2,1,0:T(8,128)} %copy.10, f32[64,64,128]{2,1,0:T(8,128)S(1)} %copy-done, f32[64,64,4]{2,1,0:T(8,128)} %copy.9), kind=kLoop, calls=%fused_computation.25 | loop fusion | flops 1114112 | bytes 4456448 | tf_op jit(solution)/shard_map/concatenate | solution.py:15
  23.9 4.3 %collective-permute-start.2 = (f32[4,64,136]{2,1,0:T(8,128)S(1)}, f32[4,64,136]{2,1,0:T(8,128)S(1)}, u32[]{:S(2)}, u32[]{:S(2)}) collective-permute-start(f32[4,64,136]{2,1,0:T(8,128)S(1)} %get-tuple-element.35), channel_id=1, source_target_pairs={{0,1},{1,2},{2,3},{4,5},{5,6},{6,7},{8,9},{9,10},{10,11},{12,13},{... | collective-permute-start | bytes 417800 | tf_op jit(solution)/shard_map/ppermute | solution.py:17
  28.2 2.1 %collective-permute-start.3 = (f32[4,64,136]{2,1,0:T(8,128)S(1)}, f32[4,64,136]{2,1,0:T(8,128)S(1)}, u32[]{:S(2)}, u32[]{:S(2)}) collective-permute-start(f32[4,64,136]{2,1,0:T(8,128)S(1)} %get-tuple-element.36), channel_id=1, source_target_pairs={{1,0},{2,1},{3,2},{5,4},{6,5},{7,6},{9,8},{10,9},{11,10},{13,12},{... | collective-permute-start | bytes 417800 | tf_op jit(solution)/shard_map/ppermute | solution.py:19
  30.3 0.7 fusion.48
  35.8 0.7 fusion.47
  36.6 5.5 %maximum_maximum_fusion = (f32[68,64,136]{2,1,0:T(8,128)S(1)}, f32[68,64,136]{2,1,0:T(8,128)}) fusion(f32[64,64,4]{2,1,0:T(8,128)S(1)} %copy-done.1, f32[64,64,128]{2,1,0:T(8,128)S(1)} %copy-done, f32[64,64,4]{2,1,0:T(8,128)S(1)} %copy-done.2, f32[4,64,136]{2,1,0:T(8,128)S(1)} %collective-permute-done.2, f32[4,64,136]{2,1,0:T(8,128)S(1)} %collective-permute-done.3), kind=kLoop, calls=%fused_computation.7 | loop fusion | flops 3551232 | bytes 7241728 | tf_op jit(solution)/shard_map/concatenate | solution.py:15
  42.1 9.7 %fusion.3 = f32[64,64,136]{2,1,0:T(8,128)S(1)} fusion(f32[68,64,136]{2,1,0:T(8,128)} %get-tuple-element.34, f32[68,64,136]{2,1,0:T(8,128)S(1)} %get-tuple-element.33, f32[64,64,4]{2,1,0:T(8,128)} %copy.10, f32[64,64,128]{2,1,0:T(8,128)S(1)} %copy-done, f32[64,64,4]{2,1,0:T(8,128)} %copy.9), kind=kLoop, calls=%fused_computation.10 | loop fusion | flops 10584064 | bytes 22282240 | tf_op jit(solution)/shard_map/add | solution.py:36
  51.9 4.5 %fusion.35 = f32[64,64,128]{2,1,0:T(8,128)S(1)} fusion(f32[64,64,136]{2,1,0:T(8,128)S(1)} %fusion.3), kind=kLoop, calls=%fused_computation.67 | loop fusion | flops 8912896 | bytes 20971520 | tf_op jit(solution)/shard_map/add | solution.py:36
  56.3 15.9 %add_multiply_fusion = (f32[64,64,128]{2,1,0:T(8,128)S(1)}, f32[64,64,128]{2,1,0:T(8,128)S(1)}) fusion(f32[]{:T(128)} %bitcast.24, f32[]{:T(128)} %bitcast.21, f32[]{:T(128)} %bitcast.18, f32[]{:T(128)} %bitcast.15, f32[]{:T(128)} %bitcast.12, f32[]{:T(128)} %bitcast.9, f32[]{:T(128)} %bitcast.6, f32[]{:T(128)} %bitcast.3, f32[]{:T(128)} %bitcast.26, ...), kind=kLoop, calls=%fused_computation.87 | loop fusion | flops 29884416 | bytes 6291552 | tf_op jit(solution)/shard_map/div | solution.py:72
  72.3 15.5 %fusion.52 = f32[64,64,128]{2,1,0:T(8,128)S(1)} fusion(f32[64,64,128]{2,1,0:T(8,128)S(1)} %get-tuple-element.29), kind=kOutput, calls=%fused_computation.98 | output fusion | flops 33030144 | bytes 4194304 | tf_op jit(solution)/shard_map/jit(cumsum)/reduce_window_sum | solution.py:73
  87.8 14.6 %multiply_reduce_fusion.2 = f32[64,128]{1,0:T(8,128)S(1)} fusion(f32[]{:T(128)} %bitcast.34, f32[]{:T(128)} %bitcast.33, f32[]{:T(128)} %bitcast.32, f32[]{:T(128)} %bitcast.31, f32[]{:T(128)} %bitcast.30, f32[]{:T(128)} %bitcast.29, f32[]{:T(128)} %bitcast.28, f32[]{:T(128)} %bitcast.27, f32[64,64,128]{2,1,0:T(8,128)S(1)} %get-tuple-element.30, ...), kind=kLoop, calls=%fused_computation.85 | loop fusion | flops 24109056 | bytes 6324320 | tf_op jit(solution)/shard_map/reduce_sum | solution.py:76
  102.4 14.9 %multiply_reduce_fusion.1 = f32[64,128]{1,0:T(8,128)S(1)} fusion(f32[]{:T(128)} %bitcast.43, f32[]{:T(128)} %bitcast.42, f32[]{:T(128)} %bitcast.41, f32[]{:T(128)} %bitcast.40, f32[]{:T(128)} %bitcast.39, f32[]{:T(128)} %bitcast.38, f32[]{:T(128)} %bitcast.37, f32[]{:T(128)} %bitcast.36, f32[64,64,128]{2,1,0:T(8,128)S(1)} %get-tuple-element.30, ...), kind=kLoop, calls=%fused_computation.84 | loop fusion | flops 24109056 | bytes 6324320 | tf_op jit(solution)/shard_map/reduce_sum | solution.py:76
  117.3 0.0 copy-start.4
  117.3 14.7 %multiply_reduce_fusion = f32[64,128]{1,0:T(8,128)S(1)} fusion(f32[]{:T(128)} %bitcast.52, f32[]{:T(128)} %bitcast.51, f32[]{:T(128)} %bitcast.50, f32[]{:T(128)} %bitcast.49, f32[]{:T(128)} %bitcast.48, f32[]{:T(128)} %bitcast.47, f32[]{:T(128)} %bitcast.46, f32[]{:T(128)} %bitcast.45, f32[64,64,128]{2,1,0:T(8,128)S(1)} %get-tuple-element.30, f32[]{:T(128)} %bitcast.26, ...), kind=kLoop, calls=%fused_computation.83 | loop fusion | flops 24109056 | bytes 6324320 | tf_op jit(solution)/shard_map/reduce_sum | solution.py:76
  132.1 0.7 pad_maximum_fusion.3
  132.7 3.4 %all-to-all-start = ((f32[4,4,16,128]{3,2,0,1:T(8,128)}), f32[4,4,16,128]{3,2,0,1:T(8,128)S(1)}, u32[]{:S(2)}, u32[]{:S(2)}) async-start(f32[4,4,16,128]{3,2,0,1:T(8,128)} %pad_maximum_fusion.3), calls=%async_computation | async-start | bytes 262144 | tf_op jit(solution)/shard_map/all_to_all | solution.py:82
  136.1 3.6 %all-to-all-done = f32[4,4,16,128]{3,2,0,1:T(8,128)S(1)} async-done(((f32[4,4,16,128]{3,2,0,1:T(8,128)}), f32[4,4,16,128]{3,2,0,1:T(8,128)S(1)}, u32[]{:S(2)}, u32[]{:S(2)}) %all-to-all-start) | async-done | bytes 131104 | tf_op jit(solution)/shard_map/all_to_all | solution.py:82
  139.7 0.2 while.10
  140.0 0.0 copy-start.3
  140.0 0.6 copy-done.3
  (31 shorter events, 0.2 us)
Async XLA Ops:
  4.4 9.0 %copy-start.6 = (f32[8]{0:T(128)S(1)}, f32[8]{0:T(128)}, u32[]{:S(2)}) copy-start(f32[8]{0:T(128)} %param.9) | copy-start | bytes 100
  4.4 9.6 %copy-start.7 = (f32[8]{0:T(128)S(1)}, f32[8]{0:T(128)}, u32[]{:S(2)}) copy-start(f32[8]{0:T(128)} %param.8) | copy-start | bytes 100
  4.4 10.3 %copy-start.8 = (f32[8]{0:T(128)S(1)}, f32[8]{0:T(128)}, u32[]{:S(2)}) copy-start(f32[8]{0:T(128)} %param.10) | copy-start | bytes 100
  6.7 8.6 %collective-permute-start.1 = (f32[64,64,4]{1,0,2:T(8,128)S(1)}, f32[64,64,4]{1,0,2:T(8,128)S(1)}, u32[]{:S(2)}, u32[]{:S(2)}) collective-permute-start(f32[64,64,4]{1,0,2:T(8,128)S(1)} %copy.13), channel_id=1, source_target_pairs={{4,0},{8,4},{12,8},{16,12},{20,16},{24,20},{28,24},{5,1},{9,5},{13... | collective-permute-start | bytes 196616 | tf_op jit(solution)/shard_map/ppermute | solution.py:19
  8.8 8.9 %collective-permute-start = (f32[64,64,4]{1,0,2:T(8,128)S(1)}, f32[64,64,4]{1,0,2:T(8,128)S(1)}, u32[]{:S(2)}, u32[]{:S(2)}) collective-permute-start(f32[64,64,4]{1,0,2:T(8,128)S(1)} %copy.12), channel_id=1, source_target_pairs={{0,4},{4,8},{8,12},{12,16},{16,20},{20,24},{24,28},{1,5},{5,9},{9,... | collective-permute-start | bytes 196616 | tf_op jit(solution)/shard_map/ppermute | solution.py:17
  15.4 4.4 %copy-start = (f32[64,64,128]{2,1,0:T(8,128)S(1)}, f32[64,64,128]{2,1,0:T(8,128)}, u32[]{:S(2)}) copy-start(f32[64,64,128]{2,1,0:T(8,128)} %param.7) | copy-start | bytes 6291460
  19.8 10.5 %copy-start.5 = (f32[3,8]{1,0:T(4,128)S(1)}, f32[3,8]{1,0:T(4,128)}, u32[]{:S(2)}) copy-start(f32[3,8]{1,0:T(4,128)} %param.11) | copy-start | bytes 292
  19.8 16.8 %copy-start.1 = (f32[64,64,4]{2,1,0:T(8,128)S(1)}, f32[64,64,4]{2,1,0:T(8,128)}, u32[]{:S(2)}) copy-start(f32[64,64,4]{2,1,0:T(8,128)} %copy.10) | copy-start | bytes 196612
  19.8 16.8 %copy-start.2 = (f32[64,64,4]{2,1,0:T(8,128)S(1)}, f32[64,64,4]{2,1,0:T(8,128)}, u32[]{:S(2)}) copy-start(f32[64,64,4]{2,1,0:T(8,128)} %copy.9) | copy-start | bytes 196612
  23.9 12.7 %collective-permute-start.2 = (f32[4,64,136]{2,1,0:T(8,128)S(1)}, f32[4,64,136]{2,1,0:T(8,128)S(1)}, u32[]{:S(2)}, u32[]{:S(2)}) collective-permute-start(f32[4,64,136]{2,1,0:T(8,128)S(1)} %get-tuple-element.35), channel_id=1, source_target_pairs={{0,1},{1,2},{2,3},{4,5},{5,6},{6,7},{8,9},{9,10},{10,11},{12,13},{... | collective-permute-start | bytes 417800 | tf_op jit(solution)/shard_map/ppermute | solution.py:17
  28.2 8.4 %collective-permute-start.3 = (f32[4,64,136]{2,1,0:T(8,128)S(1)}, f32[4,64,136]{2,1,0:T(8,128)S(1)}, u32[]{:S(2)}, u32[]{:S(2)}) collective-permute-start(f32[4,64,136]{2,1,0:T(8,128)S(1)} %get-tuple-element.36), channel_id=1, source_target_pairs={{1,0},{2,1},{3,2},{5,4},{6,5},{7,6},{9,8},{10,9},{11,10},{13,12},{... | collective-permute-start | bytes 417800 | tf_op jit(solution)/shard_map/ppermute | solution.py:19
  117.3 22.4 %copy-start.4 = (f32[4,16,128]{2,1,0:T(8,128)S(1)}, f32[4,16,128]{2,1,0:T(8,128)}, u32[]{:S(2)}) copy-start(f32[4,16,128]{2,1,0:T(8,128)} %constant.16.clone.1) | copy-start | bytes 98308
  132.7 7.0 %all-to-all-start = ((f32[4,4,16,128]{3,2,0,1:T(8,128)}), f32[4,4,16,128]{3,2,0,1:T(8,128)S(1)}, u32[]{:S(2)}, u32[]{:S(2)}) async-start(f32[4,4,16,128]{3,2,0,1:T(8,128)} %pad_maximum_fusion.3), calls=%async_computation | async-start | bytes 262144 | tf_op jit(solution)/shard_map/all_to_all | solution.py:82
  140.0 0.6 copy-start.3
where the time goes:
time: 143 us; the launch traced here: 141 us
  other arithmetic  100 us (70%)
  local copies, waits for them, and re-layouts  15.7 us (11%)
  starting transfers between devices  15.7 us (11%)
  between operations  5.04 us (4%)
  waiting for transfers between devices  3.77 us (3%)
    reduce_sum x3, other arithmetic, on_device(): planes = [jnp.sum(weight * emits[chan], axis=0) for chan in range(3)]  44.2 us
    div x1, other arithmetic, on_device(): tau = sigma / jnp.float32(depth_cells * lax.axis_size('gz'))  15.9 us
    another operation x1, other arithmetic, on_device(): cumul = jnp.cumsum(tau, axis=0)  15.5 us
    add x2, other arithmetic, valid_pass(): total + weights[offset] * lax.slice_in_dim(field, offset, offset + count,...  14.2 us
    concatenate x2, other arithmetic, padded_2(): jnp.concatenate([lax.ppermute(tail, axis, [(i, (i + 1) % count) for i in...  9.59 us
    ppermute x2, starting transfers between devices, padded_2(): lax.ppermute(tail, axis, [(i, (i + 1) % count) for i in range(ends)])  8.91 us
    slice x2, local copies, waits for them, and re-layouts, padded_2(): lax.slice_in_dim(cells, cells.shape[dim] - width, cells.shape[dim], axis=...  4.45 us
    unnamed x20, local copies, waits for them, and re-layouts  3.68 us
  transfers between devices with their start and end apart: 5, of which 2 were waited for; matrix products, arithmetic and copies ran while one was open for 4% of the time, Pallas kernels for 0%

commit v1 on v0

v1 whole, which is shorter than its diff:
```python
import functools
import math

import jax
import jax.numpy as jnp
import numpy as np
from jax import lax
from jax.experimental import pallas as pl
from jax.experimental.pallas import tpu as pltpu
from jax.sharding import PartitionSpec as P

F32 = jnp.float32
BF16 = jnp.bfloat16
MESH = pl.DeviceIdType.MESH
HALO = 4
PIECE = 2 * HALO


def tap_weights():
    raw = [math.exp(-(j * j) / 8.0) for j in range(-4, 5)]
    whole = sum(raw)
    return [value / whole for value in raw]


def split_const(matrix):
    high = matrix.astype(np.float32).astype(BF16)
    low = (matrix - high.astype(np.float64)).astype(np.float32).astype(BF16)
    return high, low


def band(count, shift, rows):
    weights = tap_weights()
    matrix = np.zeros((rows, count), np.float64)
    for source in range(rows):
        for target in range(count):
            offset = shift(source) - target
            if -4 <= offset <= 4:
                matrix[source, target] = weights[offset + 4]
    return matrix


def constants(rows, columns):
    high, low = split_const(band(rows, lambda i: i, rows).T)
    left = np.concatenate([high, high, low], axis=1)
    high, low = split_const(band(columns, lambda i: i, columns))
    main = np.concatenate([high, high, low], axis=0)
    side = np.zeros((columns, columns), np.float64)
    side[:PIECE] = band(columns, lambda i: i - HALO if i < HALO else columns + i - HALO, PIECE)
    high, low = split_const(side)
    edge = np.concatenate([high, high, low], axis=0)
    return left, main, edge


def split(value):
    high = value.astype(BF16)
    low = (value - high.astype(F32)).astype(BF16)
    return high, low


def rows_pass(left, slab):
    high, low = split(slab)
    return jnp.dot(left, jnp.concatenate([high, low, high], axis=0), preferred_element_type=F32)


def columns_pass(rows, matrix):
    high, low = split(rows)
    return jnp.dot(jnp.concatenate([high, low, high], axis=1), matrix, preferred_element_type=F32)


def kernel(nx, nz, terms, volume, centers, sharpness, extinction, colors, left_ref, main_ref, edge_ref,
           out_ref, vol, packed, from_left, from_right, layers, smooth, sent, pieces,
           load_sem, left_send, left_recv, right_send, right_recv, layer_send, layer_recv, image_send, image_recv):
    depth, rows, columns = vol.shape
    per_group = columns // PIECE
    groups = depth // per_group
    row_block = rows // nz
    ix = lax.axis_index("gx")
    iz = lax.axis_index("gz")
    has_left, has_right = ix > 0, ix < nx - 1
    has_front, has_back = iz > 0, iz < nz - 1

    barrier = pltpu.get_barrier_semaphore()

    def greet(x, z):
        pl.semaphore_signal(barrier, inc=1, device_id={"gx": x, "gz": z}, device_id_type=MESH)

    loads = []
    for g in range(groups):
        span = pl.ds(g * per_group, per_group)
        loads.append(pltpu.make_async_copy(volume.at[span], vol.at[span], load_sem.at[g]))
        loads[-1].start()

    for step in range(1, nz):
        greet(ix, lax.rem(iz + step, nz))
    for here, x in ((has_left, ix - 1), (has_right, ix + 1)):
        pl.when(here)(functools.partial(greet, x, iz))
        pl.when(here & has_front)(functools.partial(greet, x, iz - 1))
        pl.when(here & has_back)(functools.partial(greet, x, iz + 1))
    sides = has_left.astype(jnp.int32) + has_right.astype(jnp.int32)
    ends = has_front.astype(jnp.int32) + has_back.astype(jnp.int32)

    lane = lax.broadcasted_iota(jnp.int32, (rows, columns), 1)

    def pack(g):
        def body(m, total):
            turned = pltpu.roll(vol[g * per_group + m], lax.rem(PIECE * m + HALO, columns), axis=1)
            return jnp.where(lane // PIECE == m, turned, total)

        total = jnp.zeros((rows, columns), F32)
        for m in range(per_group):
            total = body(m, total)
        packed[g] = total

    def remote(source, target, send, recv, x, z):
        return pltpu.make_async_remote_copy(
            src_ref=source, dst_ref=target, send_sem=send, recv_sem=recv,
            device_id={"gx": x, "gz": z}, device_id_type=MESH,
        )

    last = groups - 1
    copies = []

    def launch(condition, copy):
        copies.append((condition, copy))
        pl.when(condition)(copy.start)

    for g in range(groups):
        loads[g].wait()
        pack(g)
        if g == 0:
            pl.semaphore_wait(barrier, nz - 1 + sides * (1 + ends))
        for here, x, inbox, send, recv in (
            (has_right, ix + 1, from_left, left_send, left_recv),
            (has_left, ix - 1, from_right, right_send, right_recv),
        ):
            launch(here, remote(packed.at[g], inbox.at[g + 1], send.at[g + 1], recv.at[g + 1], x, iz))
            if g == 0:
                slot = groups + 1
                launch(here & has_front, remote(packed.at[0], inbox.at[slot], send.at[slot], recv.at[slot], x, iz - 1))
            if g == last:
                launch(here & has_back, remote(packed.at[last], inbox.at[0], send.at[0], recv.at[0], x, iz + 1))
        if g == 0:
            launch(has_back, remote(volume.at[pl.ds(depth - HALO, HALO)], layers.at[0], layer_send.at[0], layer_recv.at[0], ix, iz + 1))
            launch(has_front, remote(volume.at[pl.ds(0, HALO)], layers.at[1], layer_send.at[1], layer_recv.at[1], ix, iz - 1))

    left = left_ref[...]

    def plane_pass(source, start, target):
        wide = jnp.concatenate([source[start + i] for i in range(HALO)], axis=1)
        wide = rows_pass(left, wide)
        tall = jnp.concatenate([wide[:, i * columns:(i + 1) * columns] for i in range(HALO)], axis=0)
        tall = columns_pass(tall, main_ref[...])
        for i in range(HALO):
            smooth[target + i] = tall[i * rows:(i + 1) * rows]

    @pl.loop(0, depth // HALO)
    def _(step):
        plane_pass(vol, step * HALO, step * HALO + HALO)

    def arrive(condition, copy, inbox):
        pl.when(condition)(copy.wait_recv)

        @pl.when(jnp.logical_not(condition))
        def _():
            inbox[...] = jnp.zeros(inbox.shape, F32)

    for end, here in ((0, has_front), (1, has_back)):
        arrive(here, remote(layers.at[end], layers.at[end], layer_send.at[end], layer_recv.at[end], ix, iz), layers.at[end])
        plane_pass(layers.at[end], 0, end * (depth + HALO))

    for g in range(groups + 2):
        beside = has_front if g == 0 else has_back if g == groups + 1 else None
        for here, inbox, send, recv in (
            (has_left, from_left, left_send, left_recv),
            (has_right, from_right, right_send, right_recv),
        ):
            both = here if beside is None else here & beside
            arrive(both, remote(inbox.at[g], inbox.at[g], send.at[g], recv.at[g], ix, iz), inbox.at[g])

    def edges(g, first, count, target):
        piece = jnp.where(lane % PIECE < HALO, from_left[g], from_right[g])
        piece = rows_pass(left, piece)
        for m in range(first, first + count, HALO):
            tall = jnp.concatenate(
                [pltpu.roll(piece, (columns - PIECE * (m + i)) % columns, axis=1) for i in range(HALO)], axis=0
            )
            tall = columns_pass(tall, edge_ref[...])
            for i in range(HALO):
                at = target + m - first + i
                smooth[at] = smooth[at] + tall[i * rows:(i + 1) * rows]

    edges(0, per_group - HALO, HALO, 0)
    edges(groups + 1, 0, HALO, depth + HALO)

    @pl.loop(0, groups)
    def _(g):
        edges(g + 1, 0, per_group, g * per_group + HALO)

    taps = tap_weights()
    comps = centers.shape[0]
    log2e = math.log2(math.e)
    cells = depth * nz
    middle = [centers[k] for k in range(comps)]
    fall = [sharpness[k] * F32(-log2e) for k in range(comps)]
    absorb = [extinction[k] * F32(1.0 / cells) for k in range(comps)]
    shine = [[colors[c, k] for k in range(comps)] for c in range(3)]
    unroll = 2

    def render(row):
        start = pl.multiple_of(row * row_block, row_block)

        def body(step, carry):
            trans, red, green, blue = carry
            z = step * unroll

            def load(j):
                return smooth[pl.ds(z + j, unroll), pl.ds(start, row_block), :]

            density = taps[4] * load(4)
            for j in range(4):
                density = density + taps[j] * (load(j) + load(8 - j))
            tau = None
            for k in range(comps):
                offset = density - middle[k]
                bump = jnp.exp2(fall[k] * offset * offset)
                if tau is None:
                    tau = absorb[k] * bump
                    emits = [shine[c][k] * bump for c in range(3)]
                else:
                    tau = tau + absorb[k] * bump
                    emits = [emits[c] + shine[c][k] * bump for c in range(3)]
            series = tau * ((-1.0) ** (terms - 1) / math.factorial(terms))
            for n in range(terms - 1, 0, -1):
                series = (series + (-1.0) ** (n - 1) / math.factorial(n)) * tau
            for i in range(unroll):
                weight = trans * series[i]
                trans = trans - weight
                red = red + weight * emits[0][i]
                green = green + weight * emits[1][i]
                blue = blue + weight * emits[2][i]
            return trans, red, green, blue

        none = jnp.zeros((row_block, columns), F32)
        trans, red, green, blue = lax.fori_loop(0, depth // unroll, body, (none + 1.0, none, none, none))
        return red, green, blue, trans

    for step in range(1, nz):
        peer = lax.rem(iz + step, nz)
        for c, plane in enumerate(render(peer)):
            sent[step - 1, c] = plane
        copy = remote(sent.at[step - 1], pieces.at[iz], image_send.at[step - 1], image_recv.at[iz], ix, peer)
        copy.start()
        copies.append((None, copy))
    for c, plane in enumerate(render(iz)):
        pieces[iz, c] = plane

    for step in range(1, nz):
        peer = lax.rem(iz + step, nz)
        remote(pieces.at[peer], pieces.at[peer], image_send.at[step - 1], image_recv.at[peer], ix, peer).wait_recv()

    color = [pieces[0, c] for c in range(3)]
    trans = pieces[0, 3]
    for n in range(1, nz):
        color = [color[c] + trans * pieces[n, c] for c in range(3)]
        trans = trans * pieces[n, 3]
    for c in range(3):
        out_ref[c] = color[c]
    out_ref[3] = trans

    for condition, copy in copies:
        if condition is None:
            copy.wait_send()
        else:
            pl.when(condition)(copy.wait_send)


def on_device(volume, centers, sharpness, extinction, colors):
    nx, nz = lax.axis_size("gx"), lax.axis_size("gz")
    depth, rows, columns = volume.shape
    groups = depth // (columns // PIECE)
    row_block = rows // nz
    bound = 3.0 * centers.shape[0] / (depth * nz)
    terms = 1
    while bound ** terms / math.factorial(terms + 1) > 2.0 ** -26:
        terms += 1
    left, main, edge = constants(rows, columns)
    smem = pl.BlockSpec(memory_space=pltpu.SMEM)
    vmem = pl.BlockSpec(memory_space=pltpu.VMEM)
    dma = pltpu.SemaphoreType.DMA
    slab = (rows, columns)
    return pl.pallas_call(
        functools.partial(kernel, nx, nz, terms),
        out_shape=jax.ShapeDtypeStruct((4, row_block, columns), F32),
        in_specs=[pl.BlockSpec(memory_space=pl.ANY)] + [smem] * 4 + [vmem] * 3,
        out_specs=vmem,
        scratch_shapes=[
            pltpu.VMEM((depth,) + slab, F32),
            pltpu.VMEM((groups,) + slab, F32),
            pltpu.VMEM((groups + 2,) + slab, F32),
            pltpu.VMEM((groups + 2,) + slab, F32),
            pltpu.VMEM((2, HALO) + slab, F32),
            pltpu.VMEM((depth + 2 * HALO,) + slab, F32),
            pltpu.VMEM((nz - 1, 4, row_block, columns), F32),
            pltpu.VMEM((nz, 4, row_block, columns), F32),
            dma((groups,)),
            dma((groups + 2,)), dma((groups + 2,)),
            dma((groups + 2,)), dma((groups + 2,)),
            dma((2,)), dma((2,)),
            dma((nz - 1,)), dma((nz,)),
        ],
        compiler_params=pltpu.CompilerParams(
            collective_id=0, has_side_effects=True, vmem_limit_bytes=32 * 1024 * 1024
        ),
    )(volume, centers, sharpness, extinction, colors, jnp.asarray(left), jnp.asarray(main), jnp.asarray(edge))


def solution(mesh):
    return jax.shard_map(
        on_device,
        mesh=mesh,
        in_specs=(P("gz", None, "gx"), P(), P(), P(), P()),
        out_specs=P(None, "gz", "gx"),
        check_vma=False,
    )
```

time: 143 us -> 33.3 us (0.23)
  the two profiles are of different devices: /device:TPU:1 before, /device:TPU:17 now
where the time goes in v1:
time: 33.3 us; the launch traced here: 32.9 us
  Pallas kernels  25.5 us (77%)
  local copies, waits for them, and re-layouts  7.39 us (22%)
    pallas_call x1, Pallas kernels, on_device(): pl.pallas_call(functools.partial(kernel, nx, nz, terms), out_shape=jax.Sh...  25.5 us
    unnamed x17, local copies, waits for them, and re-layouts  7.39 us

profile of v1, /device:TPU:17, one launch (start us, length us, event | category | flops | bytes accessed | tf_op | source)
XLA Modules:
  0.0 32.9 jit_solution(1093138462607912345)
XLA Ops:
  0.0 0.0 copy-start
  0.0 1.6 %copy-done = f32[64,64,128]{2,1,0:T(8,128)S(1)} copy-done((f32[64,64,128]{2,1,0:T(8,128)S(1)}, f32[64,64,128]{2,1,0:T(8,128)}, u32[]{:S(2)}) %copy-start) | copy-done | bytes 2097176
  1.6 0.0 copy-start.1
  1.6 0.9 %copy-done.1 = bf16[384,128]{1,0:T(8,128)(2,1)S(1)} copy-done((bf16[384,128]{1,0:T(8,128)(2,1)S(1)}, bf16[384,128]{1,0:T(8,128)(2,1)}, u32[]{:S(2)}) %copy-start.1) | copy-done | bytes 98328
  2.5 0.0 copy-start.2
  2.5 0.9 %copy-done.2 = bf16[384,128]{1,0:T(8,128)(2,1)S(1)} copy-done((bf16[384,128]{1,0:T(8,128)(2,1)S(1)}, bf16[384,128]{1,0:T(8,128)(2,1)}, u32[]{:S(2)}) %copy-start.2) | copy-done | bytes 98328
  3.4 0.0 copy-start.3
  3.4 0.8 %copy-done.3 = bf16[64,192]{1,0:T(8,128)(2,1)S(1)} copy-done((bf16[64,192]{1,0:T(8,128)(2,1)S(1)}, bf16[64,192]{1,0:T(8,128)(2,1)}, u32[]{:S(2)}) %copy-start.3) | copy-done | bytes 24600
  4.1 0.0 copy-start.4
  4.1 0.7 %copy-done.4 = f32[3,8]{1,0:T(4,128)S(1)} copy-done((f32[3,8]{1,0:T(4,128)S(1)}, f32[3,8]{1,0:T(4,128)}, u32[]{:S(2)}) %copy-start.4) | copy-done | bytes 120
  4.8 0.0 copy-start.5
  4.8 0.7 %copy-done.5 = f32[8]{0:T(128)S(1)} copy-done((f32[8]{0:T(128)S(1)}, f32[8]{0:T(128)}, u32[]{:S(2)}) %copy-start.5) | copy-done | bytes 56
  5.5 0.0 copy-start.6
  5.5 0.7 %copy-done.6 = f32[8]{0:T(128)S(1)} copy-done((f32[8]{0:T(128)S(1)}, f32[8]{0:T(128)}, u32[]{:S(2)}) %copy-start.6) | copy-done | bytes 56
  6.1 0.0 copy-start.7
  6.1 0.7 %copy-done.7 = f32[8]{0:T(128)S(1)} copy-done((f32[8]{0:T(128)S(1)}, f32[8]{0:T(128)}, u32[]{:S(2)}) %copy-start.7) | copy-done | bytes 56
  6.8 25.5 %shard_map.82 = f32[4,16,128]{2,1,0:T(8,128)S(1)} custom-call(f32[64,64,128]{2,1,0:T(8,128)S(1)} %copy-done, f32[8]{0:T(128)S(1)} %copy-done.5, f32[8]{0:T(128)S(1)} %copy-done.6, f32[8]{0:T(128)S(1)} %copy-done.7, f32[3,8]{1,0:T(4,128)S(1)} %copy-done.4, bf16[64,192]{1,0:T(8,128)(2,1)S(1)} %copy-done.3, bf16[384,128]{1,0:T(8,128)(2,1)S(1)} %copy-done.2, ...), custom_call_target="tpu_custom_call" | custom-call | tf_op jit(solution)/shard_map/pallas_call | solution.py:291
  32.3 0.6 %copy.10 = f32[4,16,128]{2,1,0:T(8,128)} copy(f32[4,16,128]{2,1,0:T(8,128)S(1)} %shard_map.82) | data formatting | bytes 65536
Async XLA Ops:
  0.0 1.6 %copy-start = (f32[64,64,128]{2,1,0:T(8,128)S(1)}, f32[64,64,128]{2,1,0:T(8,128)}, u32[]{:S(2)}) copy-start(f32[64,64,128]{2,1,0:T(8,128)} %volume.1) | copy-start | bytes 6291460
  1.6 0.9 %copy-start.1 = (bf16[384,128]{1,0:T(8,128)(2,1)S(1)}, bf16[384,128]{1,0:T(8,128)(2,1)}, u32[]{:S(2)}) copy-start(bf16[384,128]{1,0:T(8,128)(2,1)} %constant.8.clone.edge_ref) | copy-start | bytes 294916
  2.5 0.9 %copy-start.2 = (bf16[384,128]{1,0:T(8,128)(2,1)S(1)}, bf16[384,128]{1,0:T(8,128)(2,1)}, u32[]{:S(2)}) copy-start(bf16[384,128]{1,0:T(8,128)(2,1)} %constant.7.clone.main_ref) | copy-start | bytes 294916
  3.4 0.8 %copy-start.3 = (bf16[64,192]{1,0:T(8,128)(2,1)S(1)}, bf16[64,192]{1,0:T(8,128)(2,1)}, u32[]{:S(2)}) copy-start(bf16[64,192]{1,0:T(8,128)(2,1)} %constant.6.clone.left_ref) | copy-start | bytes 73732
  4.1 0.7 %copy-start.4 = (f32[3,8]{1,0:T(4,128)S(1)}, f32[3,8]{1,0:T(4,128)}, u32[]{:S(2)}) copy-start(f32[3,8]{1,0:T(4,128)} %colors.1) | copy-start | bytes 292
  4.8 0.7 %copy-start.5 = (f32[8]{0:T(128)S(1)}, f32[8]{0:T(128)}, u32[]{:S(2)}) copy-start(f32[8]{0:T(128)} %centers.1) | copy-start | bytes 100
  5.5 0.7 %copy-start.6 = (f32[8]{0:T(128)S(1)}, f32[8]{0:T(128)}, u32[]{:S(2)}) copy-start(f32[8]{0:T(128)} %sharpness.1) | copy-start | bytes 100
  6.1 0.7 %copy-start.7 = (f32[8]{0:T(128)S(1)}, f32[8]{0:T(128)}, u32[]{:S(2)}) copy-start(f32[8]{0:T(128)} %extinction.1) | copy-start | bytes 100

commit v2 on v1

v2 whole, which is shorter than its diff:
```python
import functools
import math

import jax
import jax.numpy as jnp
import numpy as np
from jax import lax
from jax.experimental import pallas as pl
from jax.experimental.pallas import tpu as pltpu
from jax.sharding import PartitionSpec as P

F32 = jnp.float32
BF16 = jnp.bfloat16
MESH = pl.DeviceIdType.MESH
HALO = 4


def tap_weights():
    raw = [math.exp(-(j * j) / 8.0) for j in range(-4, 5)]
    whole = sum(raw)
    return [value / whole for value in raw]


def split_const(matrix):
    high = matrix.astype(np.float32).astype(BF16)
    low = (matrix - high.astype(np.float64)).astype(np.float32).astype(BF16)
    return high, low


def band(count, shift, rows):
    weights = tap_weights()
    matrix = np.zeros((rows, count), np.float64)
    for source in range(rows):
        for target in range(count):
            offset = shift(source) - target
            if -4 <= offset <= 4:
                matrix[source, target] = weights[offset + 4]
    return matrix


def constants(rows, columns):
    high, low = split_const(band(rows, lambda i: i, rows).T)
    left = np.concatenate([high, high, low], axis=1)
    high, low = split_const(band(columns, lambda i: i, columns))
    main = np.concatenate([high, high, low], axis=0)
    side = band(columns, lambda i: i - HALO if i < HALO else columns + i - HALO, 2 * HALO)
    half = columns // 2
    edges = []
    for m in range(half // HALO):
        spot = np.zeros((columns, columns), np.float64)
        spot[HALO * m:HALO * (m + 1)] = side[:HALO]
        spot[half + HALO * m:half + HALO * (m + 1)] = side[HALO:]
        high, low = split_const(spot)
        edges.append(np.concatenate([high, high, low], axis=0))
    edge = np.stack([np.concatenate(edges[m:m + 2], axis=1) for m in range(0, len(edges), 2)])
    return left, main, edge


def split(value):
    high = value.astype(BF16)
    low = (value - high.astype(F32)).astype(BF16)
    return high, low


def rows_pass(left, slab):
    high, low = split(slab)
    return jnp.dot(left, jnp.concatenate([high, low, high], axis=0), preferred_element_type=F32)


def columns_pass(rows, matrix):
    high, low = split(rows)
    return jnp.dot(jnp.concatenate([high, low, high], axis=1), matrix, preferred_element_type=F32)


def kernel(nx, nz, terms, volume, centers_in, sharpness_in, extinction_in, colors_in, left_in, main_in, edge_in,
           out_ref, centers, sharpness, extinction, colors, left_ref, main_ref, edge_ref, vol, packed, corner,
           beside, corner_in, layers, tall_ref, smooth, sent, pieces, load_sem, small_sem,
           beside_send, beside_recv, corner_send, corner_recv, layer_send, layer_recv, image_send, image_recv):
    depth, rows, columns = vol.shape
    per_group = columns // HALO
    groups = depth // per_group
    half = columns // 2
    row_block = rows // nz
    ix = lax.axis_index("gx")
    iz = lax.axis_index("gz")
    sides = ((ix < nx - 1, ix + 1), (ix > 0, ix - 1))
    ends = ((iz > 0, iz - 1), (iz < nz - 1, iz + 1))

    loads = []
    chunk = per_group // 2
    for g in range(2 * groups):
        span = pl.ds(g * chunk, chunk)
        loads.append(pltpu.make_async_copy(volume.at[span], vol.at[span], load_sem.at[g]))
        loads[-1].start()

    barrier = pltpu.get_barrier_semaphore()

    def greet(x, z):
        pl.semaphore_signal(barrier, inc=1, device_id={"gx": x, "gz": z}, device_id_type=MESH)

    for here, x in sides:
        pl.when(here)(functools.partial(greet, x, iz))
        for there, z in ends:
            pl.when(here & there)(functools.partial(greet, x, z))
    for step in range(1, nz):
        greet(ix, lax.rem(iz + step, nz))

    smalls = []
    for i, (source, target) in enumerate((
        (left_in, left_ref), (main_in, main_ref), (edge_in, edge_ref), (centers_in, centers),
        (sharpness_in, sharpness), (extinction_in, extinction), (colors_in, colors),
    )):
        smalls.append(pltpu.make_async_copy(source, target, small_sem.at[i]))
        smalls[-1].start()

    lane = lax.broadcasted_iota(jnp.int32, (rows, columns), 1)
    lane8 = lax.broadcasted_iota(jnp.int32, (8, columns), 1)
    corner_lanes = HALO * HALO

    def remote(source, target, send, recv, x, z):
        return pltpu.make_async_remote_copy(
            src_ref=source, dst_ref=target, send_sem=send, recv_sem=recv,
            device_id={"gx": x, "gz": z}, device_id_type=MESH,
        )

    def arrival(target, send, recv):
        return remote(target, target, send, recv, ix, iz)

    copies = []

    def launch(condition, copy):
        copies.append((condition, copy))
        pl.when(condition)(copy.start)

    for g in range(groups):
        totals = [jnp.zeros((rows, columns), F32)] * 2
        for m in range(per_group):
            if m % chunk == 0:
                loads[(g * per_group + m) // chunk].wait()
            plane = vol[g * per_group + m]
            for side, shift in ((0, HALO * m + HALO), (1, HALO * m)):
                shift = shift % columns
                turned = pltpu.roll(plane, shift, axis=1) if shift else plane
                totals[side] = jnp.where(lane // HALO == m, turned, totals[side])
        for side in range(2):
            packed[side, g] = totals[side]
        if g == 0:
            count = nz - 1
            for here, x in sides:
                span = 1 + ends[0][0].astype(jnp.int32) + ends[1][0].astype(jnp.int32)
                count = count + here.astype(jnp.int32) * span
            pl.semaphore_wait(barrier, count)
        for side, (here, x) in enumerate(sides):
            launch(here, remote(packed.at[side, g], beside.at[side, g], beside_send.at[side, g], beside_recv.at[side, g], x, iz))
        if g == 0:
            for end, (there, z) in enumerate(ends):
                edge_span = pl.ds(0 if end == 0 else depth - HALO, HALO)
                launch(there, remote(volume.at[edge_span], layers.at[1 - end], layer_send.at[end], layer_recv.at[1 - end], ix, z))
        for end, (there, z) in enumerate(ends):
            if g != (0 if end == 0 else groups - 1):
                continue
            first = 0 if end == 0 else columns - corner_lanes
            for side, (here, x) in enumerate(sides):
                small = jnp.zeros((8, columns), F32)
                for t in range(rows // 8):
                    shift = (corner_lanes * t - first) % columns
                    turned = totals[side][8 * t:8 * t + 8]
                    turned = pltpu.roll(turned, shift, axis=1) if shift else turned
                    small = jnp.where(lane8 // corner_lanes == t, turned, small)
                corner[side, end] = small
                launch(here & there, remote(
                    corner.at[side, end], corner_in.at[side, 1 - end],
                    corner_send.at[side, end], corner_recv.at[side, 1 - end], x, z,
                ))

    for small in smalls:
        small.wait()
    left = left_ref[...]

    def plane_pass(source, start, target):
        wide = jnp.concatenate([source[start + i] for i in range(HALO)], axis=1)
        wide = rows_pass(left, wide)
        tall = jnp.concatenate([wide[:, i * columns:(i + 1) * columns] for i in range(HALO)], axis=0)
        tall = columns_pass(tall, main_ref[...])
        for i in range(HALO):
            smooth[target + i] = tall[i * rows:(i + 1) * rows]

    @pl.loop(0, depth // HALO)
    def _(step):
        plane_pass(vol, step * HALO, step * HALO + HALO)

    def arrive(condition, copy, inbox):
        pl.when(condition)(copy.wait_recv)

        @pl.when(jnp.logical_not(condition))
        def _():
            inbox[...] = jnp.zeros(inbox.shape, F32)

    for end, (there, z) in enumerate(ends):
        arrive(there, arrival(layers.at[end], layer_send.at[end], layer_recv.at[end]), layers.at[end])
        plane_pass(layers.at[end], 0, end * (depth + HALO))

    for side in range(2):
        here = sides[1 - side][0]
        for g in range(groups):
            slot = (side, g)
            arrive(here, arrival(beside.at[slot], beside_send.at[slot], beside_recv.at[slot]), beside.at[slot])
        for end, (there, z) in enumerate(ends):
            slot = (side, end)
            arrive(here & there, arrival(corner_in.at[slot], corner_send.at[slot], corner_recv.at[slot]), corner_in.at[slot])

    blocks = []
    for g in range(groups):
        near, far = beside[0, g], beside[1, g]
        blocks.append(jnp.where(lane < half, near, pltpu.roll(far, half, axis=1)))
        blocks.append(jnp.where(lane < half, pltpu.roll(near, half, axis=1), far))
    for end in range(2):
        spread = []
        for t in range(rows // 8):
            shift = (columns - corner_lanes * t) % columns
            near = pltpu.roll(corner_in[0, end], shift, axis=1) if shift else corner_in[0, end]
            shift = (columns + half - corner_lanes * t) % columns
            far = pltpu.roll(corner_in[1, end], shift, axis=1) if shift else corner_in[1, end]
            spread.append(jnp.where(lane8 < half, near, far))
        blocks.append(jnp.concatenate(spread, axis=0))
    wide = rows_pass(left, jnp.concatenate(blocks, axis=1))
    high, low = split(jnp.concatenate([wide[:, i * columns:(i + 1) * columns] for i in range(len(blocks))], axis=0))
    tall_ref[...] = jnp.concatenate([high, low, high], axis=1)
    per_block = half // HALO

    def edges(pair, block, count, places):
        part = jnp.dot(tall_ref[block * rows:(block + count) * rows], edge_ref[pair], preferred_element_type=F32)
        for p, place in enumerate(places):
            for i in range(2):
                smooth[place + i] += part[p * rows:(p + 1) * rows, i * columns:(i + 1) * columns]

    for pair in range(HALO // 2):
        edges(pair, 2 * groups, 2, [2 * pair, depth + HALO + 2 * pair])

    @pl.loop(0, per_block // 2)
    def _(pair):
        edges(pair, 0, 2 * groups, [HALO + p * per_block + 2 * pair for p in range(2 * groups)])

    taps = tap_weights()
    comps = centers.shape[0]
    cells = depth * nz
    middle = [centers[k] for k in range(comps)]
    fall = [-sharpness[k] for k in range(comps)]
    absorb = [extinction[k] * F32(1.0 / cells) for k in range(comps)]
    shine = [[colors[c, k] for k in range(comps)] for c in range(3)]
    unroll = 2

    def render(row):
        start = pl.multiple_of(row * row_block, row_block)

        def body(step, carry):
            trans, red, green, blue = carry
            z = step * unroll

            def load(j):
                return smooth[pl.ds(z + j, unroll), pl.ds(start, row_block), :]

            density = taps[4] * load(4)
            for j in range(4):
                density = density + taps[j] * (load(j) + load(8 - j))
            tau = None
            for k in range(comps):
                offset = density - middle[k]
                bump = jnp.exp(fall[k] * offset * offset)
                if tau is None:
                    tau = absorb[k] * bump
                    emits = [shine[c][k] * bump for c in range(3)]
                else:
                    tau = tau + absorb[k] * bump
                    emits = [emits[c] + shine[c][k] * bump for c in range(3)]
            series = tau * ((-1.0) ** (terms - 1) / math.factorial(terms))
            for n in range(terms - 1, 0, -1):
                series = (series + (-1.0) ** (n - 1) / math.factorial(n)) * tau
            for i in range(unroll):
                weight = trans * series[i]
                trans = trans - weight
                red = red + weight * emits[0][i]
                green = green + weight * emits[1][i]
                blue = blue + weight * emits[2][i]
            return trans, red, green, blue

        none = jnp.zeros((row_block, columns), F32)
        trans, red, green, blue = lax.fori_loop(0, depth // unroll, body, (none + 1.0, none, none, none))
        return red, green, blue, trans

    for step in range(1, nz):
        peer = lax.rem(iz + step, nz)
        for c, plane in enumerate(render(peer)):
            sent[step - 1, c] = plane
        copy = remote(sent.at[step - 1], pieces.at[iz], image_send.at[step - 1], image_recv.at[iz], ix, peer)
        copy.start()
        copies.append((None, copy))
    for c, plane in enumerate(render(iz)):
        pieces[iz, c] = plane

    for step in range(1, nz):
        peer = lax.rem(iz + step, nz)
        remote(pieces.at[peer], pieces.at[peer], image_send.at[step - 1], image_recv.at[peer], ix, peer).wait_recv()

    color = [pieces[0, c] for c in range(3)]
    trans = pieces[0, 3]
    for n in range(1, nz):
        color = [color[c] + trans * pieces[n, c] for c in range(3)]
        trans = trans * pieces[n, 3]
    for c in range(3):
        out_ref[c] = color[c]
    out_ref[3] = trans

    for condition, copy in copies:
        if condition is None:
            copy.wait_send()
        else:
            pl.when(condition)(copy.wait_send)


def on_device(volume, centers, sharpness, extinction, colors):
    nx, nz = lax.axis_size("gx"), lax.axis_size("gz")
    depth, rows, columns = volume.shape
    groups = depth // (columns // HALO)
    row_block = rows // nz
    bound = 3.0 * centers.shape[0] / (depth * nz)
    terms = 1
    while bound ** terms / math.factorial(terms + 1) > 2.0 ** -26:
        terms += 1
    left, main, edge = constants(rows, columns)
    dma = pltpu.SemaphoreType.DMA
    slab = (rows, columns)
    return pl.pallas_call(
        functools.partial(kernel, nx, nz, terms),
        out_shape=jax.ShapeDtypeStruct((4, row_block, columns), F32),
        in_specs=[pl.BlockSpec(memory_space=pltpu.HBM)] * 8,
        out_specs=pl.BlockSpec(memory_space=pltpu.VMEM),
        scratch_shapes=[
            pltpu.SMEM(centers.shape, F32),
            pltpu.SMEM(sharpness.shape, F32),
            pltpu.SMEM(extinction.shape, F32),
            pltpu.SMEM(colors.shape, F32),
            pltpu.VMEM(left.shape, BF16),
            pltpu.VMEM(main.shape, BF16),
            pltpu.VMEM(edge.shape, BF16),
            pltpu.VMEM((depth,) + slab, F32),
            pltpu.VMEM((2, groups) + slab, F32),
            pltpu.VMEM((2, 2, 8, columns), F32),
            pltpu.VMEM((2, groups) + slab, F32),
            pltpu.VMEM((2, 2, 8, columns), F32),
            pltpu.VMEM((2, HALO) + slab, F32),
            pltpu.VMEM(((2 * groups + 2) * rows, 3 * columns), BF16),
            pltpu.VMEM((depth + 2 * HALO,) + slab, F32),
            pltpu.VMEM((nz - 1, 4, row_block, columns), F32),
            pltpu.VMEM((nz, 4, row_block, columns), F32),
            dma((2 * groups,)), dma((7,)),
            dma((2, groups)), dma((2, groups)),
            dma((2, 2)), dma((2, 2)),
            dma((2,)), dma((2,)),
            dma((nz - 1,)), dma((nz,)),
        ],
        compiler_params=pltpu.CompilerParams(
            collective_id=0, has_side_effects=True, vmem_limit_bytes=60 * 1024 * 1024
        ),
    )(volume, centers, sharpness, extinction, colors, jnp.asarray(left), jnp.asarray(main), jnp.asarray(edge))


def solution(mesh):
    return jax.shard_map(
        on_device,
        mesh=mesh,
        in_specs=(P("gz", None, "gx"), P(), P(), P(), P()),
        out_specs=P(None, "gz", "gx"),
        check_vma=False,
    )
```

time: 33.3 us -> 25.2 us (0.76)
  the two profiles are of different devices: /device:TPU:17 before, /device:TPU:1 now
where the time goes in v2:
time: 25.2 us; the launch traced here: 25.1 us
  Pallas kernels  23.7 us (94%)
  local copies, waits for them, and re-layouts  1.38 us (5%)
    pallas_call x1, Pallas kernels, on_device(): pl.pallas_call(functools.partial(kernel, nx, nz, terms), out_shape=jax.Sh...  23.7 us
    unnamed x1, local copies, waits for them, and re-layouts  1.38 us

profile of v2, /device:TPU:1, one launch (start us, length us, event | category | flops | bytes accessed | tf_op | source)
XLA Modules:
  0.0 25.1 jit_solution(5174144734607951333)
XLA Ops:
  0.0 23.7 %shard_map.82 = f32[4,16,128]{2,1,0:T(8,128)} custom-call(f32[64,64,128]{2,1,0:T(8,128)} %volume.1, f32[8]{0:T(128)} %centers_in.1, f32[8]{0:T(128)} %sharpness_in.1, f32[8]{0:T(128)} %extinction_in.1, f32[3,8]{1,0:T(4,128)} %colors_in.1, bf16[64,192]{1,0:T(8,128)(2,1)} %constant.6.clone.left_in, bf16[384,128]{1,0:T(8,128)(2,1)} %constant.7.clone.main_in, ...), custom_call_target="tpu_custom_call" | custom-call | tf_op jit(solution)/shard_map/pallas_call | solution.py:333
  23.7 1.4 %copy.10 = f32[4,16,128]{2,1,0:T(8,128)} copy(f32[4,16,128]{2,1,0:T(8,128)} %shard_map.82) | data formatting | bytes 65536

commit v3 on v2

--- a/solution.py
+++ b/solution.py
@@ -42,7 +42,7 @@
     high, low = split_const(band(rows, lambda i: i, rows).T)
     left = np.concatenate([high, high, low], axis=1)
     high, low = split_const(band(columns, lambda i: i, columns))
-    main = np.concatenate([high, high, low], axis=0)
+    main = np.concatenate([np.concatenate([high, high], axis=0), np.concatenate([low, low], axis=0)], axis=1)
     side = band(columns, lambda i: i - HALO if i < HALO else columns + i - HALO, 2 * HALO)
     half = columns // 2
     edges = []
@@ -69,7 +69,9 @@
 
 def columns_pass(rows, matrix):
     high, low = split(rows)
-    return jnp.dot(jnp.concatenate([high, low, high], axis=1), matrix, preferred_element_type=F32)
+    both = jnp.dot(jnp.concatenate([high, low], axis=1), matrix, preferred_element_type=F32)
+    count = both.shape[1] // 2
+    return both[:, :count] + both[:, count:]
 
 
 def kernel(nx, nz, terms, volume, centers_in, sharpness_in, extinction_in, colors_in, left_in, main_in, edge_in,
@@ -185,7 +187,7 @@
         for i in range(HALO):
             smooth[target + i] = tall[i * rows:(i + 1) * rows]
 
-    @pl.loop(0, depth // HALO)
+    @pl.loop(0, depth // HALO, unroll=8)
     def _(step):
         plane_pass(vol, step * HALO, step * HALO + HALO)
 
@@ -237,7 +239,7 @@
     for pair in range(HALO // 2):
         edges(pair, 2 * groups, 2, [2 * pair, depth + HALO + 2 * pair])
 
-    @pl.loop(0, per_block // 2)
+    @pl.loop(0, per_block // 2, unroll=8)
     def _(pair):
         edges(pair, 0, 2 * groups, [HALO + p * per_block + 2 * pair for p in range(2 * groups)])
 
@@ -248,7 +250,7 @@
     fall = [-sharpness[k] for k in range(comps)]
     absorb = [extinction[k] * F32(1.0 / cells) for k in range(comps)]
     shine = [[colors[c, k] for k in range(comps)] for c in range(3)]
-    unroll = 2
+    unroll = 4
 
     def render(row):
         start = pl.multiple_of(row * row_block, row_block)

time: 25.2 us -> 21.5 us (0.85)
  Pallas kernels: 23.7 us -> 20 us
    pallas_call x1, Pallas kernels: 23.7 us -> 20 us  [on_device(): pl.pallas_call(functools.partial(kernel, nx, nz, terms), out_shape=jax.Sh...]
where the time goes in v3:
time: 21.5 us; the launch traced here: 21.4 us
  Pallas kernels  20 us (93%)
  local copies, waits for them, and re-layouts  1.38 us (6%)
    pallas_call x1, Pallas kernels, on_device(): pl.pallas_call(functools.partial(kernel, nx, nz, terms), out_shape=jax.Sh...  20 us
    unnamed x1, local copies, waits for them, and re-layouts  1.38 us

profile of v3, /device:TPU:1, one launch (start us, length us, event | category | flops | bytes accessed | tf_op | source)
XLA Modules:
  0.0 21.4 jit_solution(3826553431675093670)
XLA Ops:
  0.0 20.0 %shard_map.82 = f32[4,16,128]{2,1,0:T(8,128)} custom-call(f32[64,64,128]{2,1,0:T(8,128)} %volume.1, f32[8]{0:T(128)} %centers_in.1, f32[8]{0:T(128)} %sharpness_in.1, f32[8]{0:T(128)} %extinction_in.1, f32[3,8]{1,0:T(4,128)} %colors_in.1, bf16[64,192]{1,0:T(8,128)(2,1)} %constant.6.clone.left_in, bf16[256,256]{1,0:T(8,128)(2,1)} %constant.7.clone.main_in, ...), custom_call_target="tpu_custom_call" | custom-call | tf_op jit(solution)/shard_map/pallas_call | solution.py:335
  20.0 1.4 %copy.10 = f32[4,16,128]{2,1,0:T(8,128)} copy(f32[4,16,128]{2,1,0:T(8,128)} %shard_map.82) | data formatting | bytes 65536

commit v4 on v3

--- a/solution.py
+++ b/solution.py
@@ -88,24 +88,24 @@
     sides = ((ix < nx - 1, ix + 1), (ix > 0, ix - 1))
     ends = ((iz > 0, iz - 1), (iz < nz - 1, iz + 1))
 
+    barrier = pltpu.get_barrier_semaphore()
+
+    def greet(x, z):
+        pl.semaphore_signal(barrier, inc=1, device_id={"gx": x, "gz": z}, device_id_type=MESH)
+
+    for here, x in sides:
+        pl.when(here)(functools.partial(greet, x, iz))
+        for there, z in ends:
+            pl.when(here & there)(functools.partial(greet, x, z))
+    for step in range(1, nz):
+        greet(ix, lax.rem(iz + step, nz))
+
     loads = []
     chunk = per_group // 2
     for g in range(2 * groups):
         span = pl.ds(g * chunk, chunk)
         loads.append(pltpu.make_async_copy(volume.at[span], vol.at[span], load_sem.at[g]))
         loads[-1].start()
-
-    barrier = pltpu.get_barrier_semaphore()
-
-    def greet(x, z):
-        pl.semaphore_signal(barrier, inc=1, device_id={"gx": x, "gz": z}, device_id_type=MESH)
-
-    for here, x in sides:
-        pl.when(here)(functools.partial(greet, x, iz))
-        for there, z in ends:
-            pl.when(here & there)(functools.partial(greet, x, z))
-    for step in range(1, nz):
-        greet(ix, lax.rem(iz + step, nz))
 
     smalls = []
     for i, (source, target) in enumerate((
@@ -247,7 +247,7 @@
     comps = centers.shape[0]
     cells = depth * nz
     middle = [centers[k] for k in range(comps)]
-    fall = [-sharpness[k] for k in range(comps)]
+    fall = [sharpness[k] * F32(-math.log2(math.e)) for k in range(comps)]
     absorb = [extinction[k] * F32(1.0 / cells) for k in range(comps)]
     shine = [[colors[c, k] for k in range(comps)] for c in range(3)]
     unroll = 4
@@ -268,7 +268,7 @@
             tau = None
             for k in range(comps):
                 offset = density - middle[k]
-                bump = jnp.exp(fall[k] * offset * offset)
+                bump = jnp.exp2(fall[k] * offset * offset)
                 if tau is None:
                     tau = absorb[k] * bump
                     emits = [shine[c][k] * bump for c in range(3)]

time: 21.5 us -> 21.2 us (0.986)
  Pallas kernels: 20 us -> 19.7 us
    pallas_call x1, Pallas kernels: 20 us -> 19.7 us  [on_device(): pl.pallas_call(functools.partial(kernel, nx, nz, terms), out_shape=jax.Sh...]
where the time goes in v4:
time: 21.2 us; the launch traced here: 21.1 us
  Pallas kernels  19.7 us (93%)
  local copies, waits for them, and re-layouts  1.38 us (7%)
    pallas_call x1, Pallas kernels, on_device(): pl.pallas_call(functools.partial(kernel, nx, nz, terms), out_shape=jax.Sh...  19.7 us
    unnamed x1, local copies, waits for them, and re-layouts  1.38 us

profile of v4, /device:TPU:1, one launch (start us, length us, event | category | flops | bytes accessed | tf_op | source)
XLA Modules:
  0.0 21.1 jit_solution(17235341123048105915)
XLA Ops:
  0.0 19.7 %shard_map.82 = f32[4,16,128]{2,1,0:T(8,128)} custom-call(f32[64,64,128]{2,1,0:T(8,128)} %volume.1, f32[8]{0:T(128)} %centers_in.1, f32[8]{0:T(128)} %sharpness_in.1, f32[8]{0:T(128)} %extinction_in.1, f32[3,8]{1,0:T(4,128)} %colors_in.1, bf16[64,192]{1,0:T(8,128)(2,1)} %constant.6.clone.left_in, bf16[256,256]{1,0:T(8,128)(2,1)} %constant.7.clone.main_in, ...), custom_call_target="tpu_custom_call" | custom-call | tf_op jit(solution)/shard_map/pallas_call | solution.py:335
  19.7 1.4 %copy.10 = f32[4,16,128]{2,1,0:T(8,128)} copy(f32[4,16,128]{2,1,0:T(8,128)} %shard_map.82) | data formatting | bytes 65536

commit v5 on v4

--- a/solution.py
+++ b/solution.py
@@ -40,7 +40,7 @@
 
 def constants(rows, columns):
     high, low = split_const(band(rows, lambda i: i, rows).T)
-    left = np.concatenate([high, high, low], axis=1)
+    left = np.concatenate([np.concatenate([high, high], axis=1), np.concatenate([low, low], axis=1)], axis=0)
     high, low = split_const(band(columns, lambda i: i, columns))
     main = np.concatenate([np.concatenate([high, high], axis=0), np.concatenate([low, low], axis=0)], axis=1)
     side = band(columns, lambda i: i - HALO if i < HALO else columns + i - HALO, 2 * HALO)
@@ -64,7 +64,9 @@
 
 def rows_pass(left, slab):
     high, low = split(slab)
-    return jnp.dot(left, jnp.concatenate([high, low, high], axis=0), preferred_element_type=F32)
+    both = jnp.dot(left, jnp.concatenate([high, low], axis=0), preferred_element_type=F32)
+    count = both.shape[0] // 2
+    return both[:count] + both[count:]
 
 
 def columns_pass(rows, matrix):

time: 21.2 us -> 21.2 us (level)
  no operation moved by 1% of the time
where the time goes in v5:
time: 21.2 us; the launch traced here: 21 us
  Pallas kernels  19.6 us (92%)
  local copies, waits for them, and re-layouts  1.38 us (7%)
    pallas_call x1, Pallas kernels, on_device(): pl.pallas_call(functools.partial(kernel, nx, nz, terms), out_shape=jax.Sh...  19.6 us
    unnamed x1, local copies, waits for them, and re-layouts  1.38 us

profile of v5, /device:TPU:1, one launch (start us, length us, event | category | flops | bytes accessed | tf_op | source)
XLA Modules:
  0.0 21.0 jit_solution(8495817338328670338)
XLA Ops:
  0.0 19.6 %shard_map.82 = f32[4,16,128]{2,1,0:T(8,128)} custom-call(f32[64,64,128]{2,1,0:T(8,128)} %volume.1, f32[8]{0:T(128)} %centers_in.1, f32[8]{0:T(128)} %sharpness_in.1, f32[8]{0:T(128)} %extinction_in.1, f32[3,8]{1,0:T(4,128)} %colors_in.1, bf16[128,128]{1,0:T(8,128)(2,1)} %constant.6.clone.left_in, bf16[256,256]{1,0:T(8,128)(2,1)} %constant.7.clone.main_in, ...), custom_call_target="tpu_custom_call" | custom-call | tf_op jit(solution)/shard_map/pallas_call | solution.py:337
  19.6 1.4 %copy.10 = f32[4,16,128]{2,1,0:T(8,128)} copy(f32[4,16,128]{2,1,0:T(8,128)} %shard_map.82) | data formatting | bytes 65536
